TPU v7x, 128 devices: a whole 4x4x4 slice. The times are simulated.
128 devices in a mesh: req: 8 (over x, core), exp: 16 (over y, z).
Axes of the slice: x: 4, y: 4, z: 4, core: 2. Of those that a mesh axis runs over, the one named last changes fastest.
Arguments:
- queries: bfloat16 [8192, 2048], P('req', 'exp'), may hold values from -6 to 6
- keys: bfloat16 [8192, 2048], P('req', 'exp'), may hold values from -15 to 15
- values: bfloat16 [8192, 2048], P('req', 'exp'), may hold values from -6 to 6
- prefix_keys: bfloat16 [4, 4096, 2048], P(None, 'req', 'exp'), may hold values from -15 to 15
- prefix_values: bfloat16 [4, 4096, 2048], P(None, 'req', 'exp'), may hold values from -6 to 6
- lengths: int32 [8, 8], P('req'), may hold values from 1 to 512, 1024 in all within a row
- groups: int32 [8, 8], P('req'), may hold values from 0 to 3
- residual: bfloat16 [8192, 2048], P(('req', 'exp')), may hold values from -6 to 6
- out_proj: bfloat16 [2048, 2048], P('exp'), may hold values from -0.125 to 0.125
- norm_gain: bfloat16 [2048], replicated, may hold values from 0.099609375 to 1.8984375
- expert_ids: int32 [8192, 4], P(('req', 'exp')), may hold values from 0 to 31, all different within a row; in each aligned block of 64 rows (0 to 63, 64 to 127, ...) at most 16 rows name the same one
- expert_gates: bfloat16 [8192, 4], P(('req', 'exp')), may hold values from 0.049804688 to 0.5
- w_gate: bfloat16 [32, 2048, 704], P('exp'), may hold values from -0.125 to 0.125
- w_up: bfloat16 [32, 2048, 704], P('exp'), may hold values from -0.125 to 0.125
- w_down: bfloat16 [32, 704, 2048], P('exp'), may hold values from -0.21875 to 0.21875
Outputs:
- layer_out: bfloat16 [8192, 2048], P(('req', 'exp'))
Inputs may be any that keep to these rules, and one draw needn't show every extreme that they name: The 8 lengths of a row sum to 1024; the longest request of each row has half of 1024 tokens. `expert_ids`: each row names 4 different experts. Among the 64 tokens of one device, no expert is named more than 16 times; on some device some expert is named exactly 16 times.
All inputs are finite; a program needn't handle non-finite values.
Results may differ from a plain program's by a relative error of at most 0.02.
Values may be sent and summed in bfloat16 or wider, within the bound.
A program may use at most 256 MiB of HBM per device.

v0:
```python
import math
import jax
import jax.numpy as jnp
from jax import lax
from jax.sharding import PartitionSpec as P

HEAD = 128
TOPK = 4
EXPERTS = 32
G = 4
RQ = 8
ROW_TOK = 1024
NEG = -1e30


def token_layout(lengths, groups):
    req_ends = jnp.cumsum(lengths, axis=-1)
    starts = req_ends - lengths
    position = jnp.arange(ROW_TOK, dtype=jnp.int32)
    request = jnp.sum((position[None, :, None] >= req_ends[:, None, :]).astype(jnp.int32), axis=-1)
    onehot = request[:, :, None] == jnp.arange(RQ, dtype=jnp.int32)[None, None, :]
    first_tok = jnp.sum(jnp.where(onehot, starts[:, None, :], 0), axis=-1)
    tok_group = jnp.sum(jnp.where(onehot, groups[:, None, :], 0), axis=-1)
    return (request, position[None, :] - first_tok, tok_group)


def split_blocks(row_count):
    if row_count % 1024 == 0 and row_count > 1024:
        return row_count // 1024
    return 1


def pack_parts(parts):
    return jnp.concatenate([parts[0], parts[1], parts[2]], axis=1)


def unpack_parts(packed, head_count):
    columns = head_count * HEAD
    return (
        packed[:, :columns],
        packed[:, columns : columns + head_count],
        packed[:, columns + head_count :],
    )


def attend_prefix(query_rows, query_group, prefix_k, prefix_v):
    row_count, columns = query_rows.shape
    head_count = columns // HEAD
    span = prefix_k.shape[1]
    key_grid = prefix_k.reshape(G, span, head_count, HEAD)
    val_grid = prefix_v.reshape(G, span, head_count, HEAD)
    blocks = split_blocks(row_count)
    block_len = row_count // blocks
    scaling = 1.0 / math.sqrt(HEAD)

    def per_block(pieces):
        block_q, block_g = pieces
        query_grid = block_q.reshape(block_len, head_count, HEAD)
        scores = (
            jnp.einsum("qhd,gkhd->hqgk", query_grid, key_grid, preferred_element_type=jnp.float32)
            * scaling
        )
        member = block_g[:, None] == jnp.arange(G, dtype=jnp.int32)[None, :]
        scores = jnp.where(member[None, :, :, None], scores, NEG)
        maxima = jnp.max(scores, axis=(2, 3))
        exp_terms = jnp.exp(scores - maxima[:, :, None, None])
        totals = jnp.sum(exp_terms, axis=(2, 3))
        weighted = jnp.einsum(
            "hqgk,gkhd->qhd",
            exp_terms.astype(jnp.bfloat16),
            val_grid,
            preferred_element_type=jnp.float32,
        )
        return (weighted.reshape(block_len, columns), maxima.T, totals.T)

    weighted, maxima, totals = lax.map(
        per_block,
        (query_rows.reshape(blocks, block_len, columns), query_group.reshape(blocks, block_len)),
    )
    return (
        weighted.reshape(row_count, columns),
        maxima.reshape(row_count, head_count),
        totals.reshape(row_count, head_count),
    )


def attend_suffix(queries, keys, values, request, position):
    row_count, columns = queries.shape
    head_count = columns // HEAD
    blocks = split_blocks(row_count)
    block_len = row_count // blocks
    scaling = 1.0 / math.sqrt(HEAD)
    key_grid = keys.reshape(row_count, head_count, HEAD)
    val_grid = values.reshape(row_count, head_count, HEAD)

    def per_block(pieces):
        block_q, block_req, block_pos = pieces
        query_grid = block_q.reshape(block_len, head_count, HEAD)
        scores = (
            jnp.einsum("qhd,khd->hqk", query_grid, key_grid, preferred_element_type=jnp.float32)
            * scaling
        )
        allowed = (request[None, :] == block_req[:, None]) & (
            position[None, :] <= block_pos[:, None]
        )
        scores = jnp.where(allowed[None, :, :], scores, NEG)
        maxima = jnp.max(scores, axis=2)
        exp_terms = jnp.exp(scores - maxima[:, :, None])
        totals = jnp.sum(exp_terms, axis=2)
        weighted = jnp.einsum(
            "hqk,khd->qhd",
            exp_terms.astype(jnp.bfloat16),
            val_grid,
            preferred_element_type=jnp.float32,
        )
        return (weighted.reshape(block_len, columns), maxima.T, totals.T)

    weighted, maxima, totals = lax.map(
        per_block,
        (
            queries.reshape(blocks, block_len, columns),
            request.reshape(blocks, block_len),
            position.reshape(blocks, block_len),
        ),
    )
    return (
        weighted.reshape(row_count, columns),
        maxima.reshape(row_count, head_count),
        totals.reshape(row_count, head_count),
    )


def combine(former, latter):
    weighted_a, maxima_a, totals_a = former
    weighted_b, maxima_b, totals_b = latter
    row_count, head_count = maxima_a.shape
    maxima = jnp.maximum(maxima_a, maxima_b)
    factor_a = jnp.exp(maxima_a - maxima)
    factor_b = jnp.exp(maxima_b - maxima)
    weighted = (
        weighted_a.reshape(row_count, head_count, HEAD) * factor_a[:, :, None]
        + weighted_b.reshape(row_count, head_count, HEAD) * factor_b[:, :, None]
    )
    return (
        weighted.reshape(row_count, head_count * HEAD),
        maxima,
        totals_a * factor_a + totals_b * factor_b,
    )


def per_device(
    queries,
    keys,
    values,
    prefix_keys,
    prefix_values,
    lengths,
    groups,
    residual,
    out_proj,
    norm_gain,
    expert_ids,
    expert_gates,
    w_gate,
    w_up,
    w_down,
):
    row_tok, columns = queries.shape
    head_count = columns // HEAD
    tok_dev = residual.shape[0]
    request, position, tok_group = token_layout(lengths, groups)
    request, position, tok_group = (request[0], position[0], tok_group[0])
    all_groups = lax.all_gather(tok_group, "req", axis=0, tiled=True)
    partial_value = pack_parts(
        attend_prefix(
            lax.all_gather(queries, "req", axis=0, tiled=True),
            all_groups,
            prefix_keys,
            prefix_values,
        )
    )
    returned = lax.all_to_all(partial_value, "req", split_axis=0, concat_axis=0, tiled=True)
    owners = returned.shape[0] // row_tok
    back_w, back_m, back_t = unpack_parts(returned, head_count)
    all_weighted = back_w.reshape(owners, row_tok, head_count, HEAD)
    all_maxima = back_m.reshape(owners, row_tok, head_count)
    all_totals = back_t.reshape(owners, row_tok, head_count)
    maxima = jnp.max(all_maxima, axis=0)
    factor = jnp.exp(all_maxima - maxima[None])
    weighted = jnp.sum(all_weighted * factor[..., None], axis=0).reshape(row_tok, columns)
    prefix_part = (weighted, maxima, jnp.sum(all_totals * factor, axis=0))
    suffix_part = attend_suffix(queries, keys, values, request, position)
    weighted, maxima, totals = combine(prefix_part, suffix_part)
    attended = (
        (weighted.reshape(row_tok, head_count, HEAD) / totals[:, :, None])
        .reshape(row_tok, columns)
        .astype(jnp.bfloat16)
    )
    exp_count = lax.axis_size("exp")
    full_proj = lax.all_gather(out_proj, "exp", axis=0, tiled=True)
    token_rows = lax.all_to_all(attended, "exp", split_axis=0, concat_axis=1, tiled=True)
    projected = jnp.dot(token_rows, full_proj, preferred_element_type=jnp.float32)
    stream = residual.astype(jnp.float32) + projected
    meansq = jnp.mean(stream * stream, axis=-1, keepdims=True)
    normed = (stream * lax.rsqrt(meansq + 1e-06) * norm_gain.astype(jnp.float32)).astype(
        jnp.bfloat16
    )
    capacity = max(2, tok_dev // 4)
    slot_count = EXPERTS * capacity
    flat_ids = expert_ids.reshape(-1)
    onehot = (flat_ids[:, None] == jnp.arange(EXPERTS, dtype=jnp.int32)[None, :]).astype(jnp.int32)
    slot_of = jnp.sum(onehot * (jnp.cumsum(onehot, axis=0) - 1), axis=1)
    dest = flat_ids * capacity + slot_of
    dest_hot = dest[:, None] == jnp.arange(slot_count, dtype=jnp.int32)[None, :]
    select = jnp.sum(dest_hot.reshape(tok_dev, TOPK, slot_count).astype(jnp.float32), axis=1)
    buffer = (
        jnp.dot(select.T.astype(jnp.bfloat16), normed, preferred_element_type=jnp.float32)
        .astype(jnp.bfloat16)
        .reshape(EXPERTS, capacity, normed.shape[1])
    )
    exp_dev = w_gate.shape[0]
    received = lax.all_to_all(buffer, "exp", split_axis=0, concat_axis=0, tiled=True)
    slots = received.shape[1]
    grid_in = received.reshape(exp_count, exp_dev, slots, received.shape[2])
    gate_h = jnp.einsum("secd,edf->secf", grid_in, w_gate, preferred_element_type=jnp.float32)
    up_h = jnp.einsum("secd,edf->secf", grid_in, w_up, preferred_element_type=jnp.float32)
    hidden = (jax.nn.silu(gate_h) * up_h).astype(jnp.bfloat16)
    expert_out = jnp.einsum("secf,efd->secd", hidden, w_down, preferred_element_type=jnp.float32)
    returned = lax.all_to_all(
        expert_out.astype(jnp.bfloat16).reshape(EXPERTS, slots, received.shape[2]),
        "exp",
        split_axis=0,
        concat_axis=0,
        tiled=True,
    )
    gates = expert_gates.astype(jnp.float32).reshape(tok_dev, TOPK, 1)
    weights = jnp.sum(
        dest_hot.reshape(tok_dev, TOPK, slot_count).astype(jnp.float32) * gates, axis=1
    )
    mixture = jnp.dot(
        weights.astype(jnp.bfloat16),
        returned.reshape(slot_count, received.shape[2]),
        preferred_element_type=jnp.float32,
    )
    return (stream + mixture).astype(jnp.bfloat16)


def solution(mesh):
    in_specs = (
        P("req", "exp"),
        P("req", "exp"),
        P("req", "exp"),
        P(None, "req", "exp"),
        P(None, "req", "exp"),
        P("req", None),
        P("req", None),
        P(("req", "exp"), None),
        P("exp", None),
        P(),
        P(("req", "exp"), None),
        P(("req", "exp"), None),
        P("exp", None, None),
        P("exp", None, None),
        P("exp", None, None),
    )
    out_specs = P(("req", "exp"), None)
    return jax.shard_map(
        per_device, mesh=mesh, in_specs=in_specs, out_specs=out_specs, check_vma=False
    )
```

profile of v0, /device:TPU:0, one launch (start us, length us, event | category | flops | bytes accessed | tf_op | source)
XLA Modules:
  0.0 288.0 jit_solution(15104359768345971016)
XLA Ops:
  6.5 0.7 all-gather.3.cloned.1.call-update
  7.3 0.7 all-gather.5.cloned.1.call-update
  8.0 0.8 reduce_window_sum.24
  8.9 0.7 subtract_bitcast_fusion
  9.6 0.8 select_reduce_fusion.2
  10.4 13.3 %all_gather.9 = s32[8192]{0:T(1024)S(1)} all-gather(s32[1024]{0:T(1024)S(1)} %get-tuple-element.81), channel_id=1, replica_groups=mesh['req'=8,'exp'=16] {'req'}, dimensions={0}, use_global_device_ids=true | all-gather | bytes 36864 | tf_op jit(solution)/shard_map/all_gather | solution.py:173
  23.6 13.1 %all-gather.3.cloned.1.call-done = bf16[8192,128]{1,0:T(8,128)(2,1)} async-done(((bf16[1024,128]{1,0:T(8,128)(2,1)}), bf16[8192,128]{1,0:T(8,128)(2,1)}) %all-gather.3.cloned.1.call-update) | async-done | bytes 2097168 | tf_op jit(solution)/shard_map/all_gather | solution.py:176
  36.7 55.3 %while.2 = (s32[]{:T(128)}, f32[8,1024,128]{1,2,0:T(8,128)}, f32[8,1024,1]{1,2,0:T(1,128)S(1)}, f32[8,1024,1]{1,2,0:T(1,128)S(1)}, s32[8,1024]{1,0:T(8,128)S(1)}...) while((s32[]{:T(128)}, f32[8,1024,128]{1,2,0:T(8,128)}, ...), condition=%wide.region_6.7_spmd, body=%wide.region_3.6_spmd.sunk | while | flops 1096812544 | bytes 29160576 | solution.py:76
  36.7 2.4 fusion.102
  39.1 1.7 fusion.104
  40.9 2.8 fusion.103
  43.6 2.4 fusion.102
  46.1 1.7 fusion.104
  47.8 2.7 fusion.103
  50.5 2.4 fusion.102
  53.0 1.7 fusion.104
  54.7 2.7 fusion.103
  57.5 2.4 fusion.102
  59.9 1.7 fusion.104
  61.6 2.7 fusion.103
  64.3 2.4 fusion.102
  66.8 1.7 fusion.104
  68.5 2.7 fusion.103
  71.2 2.4 fusion.102
  73.6 1.7 fusion.104
  75.4 2.8 fusion.103
  78.2 2.4 fusion.102
  80.6 1.7 fusion.104
  82.3 2.8 fusion.103
  85.1 2.4 fusion.102
  87.5 1.7 fusion.104
  89.2 2.8 fusion.103
  92.0 4.9 %pad_maximum_fusion = f32[8,1024,130]{1,2,0:T(8,128)} fusion(f32[8,1024,1]{1,2,0:T(1,128)S(1)} %get-tuple-element.78, f32[8,1024,1]{1,2,0:T(1,128)S(1)} %get-tuple-element.77, f32[8,1024,128]{1,2,0:T(8,128)} %get-tuple-element.76), kind=kLoop, calls=%fused_computation.27 | loop fusion | flops 2129920 | bytes 8519680 | tf_op jit(solution)/shard_map/concatenate | solution.py:34
  97.0 4.8 %all-to-all-start = ((f32[8,1024,130]{1,2,0:T(8,128)}), f32[8,1024,130]{1,2,0:T(8,128)}, u32[]{:S(2)}, u32[]{:S(2)}) async-start(f32[8,1024,130]{1,2,0:T(8,128)} %pad_maximum_fusion), calls=%async_computation | async-start | bytes 8912896 | tf_op jit(solution)/shard_map/all_to_all | solution.py:182
  101.9 0.1 eq.113
  102.0 0.1 eq.109
  102.1 0.8 reduce-window.6
  102.8 0.2 slice_reduce_fusion
  103.1 0.1 fusion.79
  103.2 0.1 reduce_sum.112
  103.4 1.1 fusion.86
  104.5 2.0 copy-done.1
  106.5 0.6 fusion.27
  107.1 47.1 %all-to-all-done = f32[8,1024,130]{1,2,0:T(8,128)} async-done(((f32[8,1024,130]{1,2,0:T(8,128)}), f32[8,1024,130]{1,2,0:T(8,128)}, u32[]{:S(2)}, u32[]{:S(2)}) %all-to-all-start) | async-done | bytes 4259872 | tf_op jit(solution)/shard_map/all_to_all | solution.py:182
  154.2 4.7 %copy.132 = f32[8,1024,130]{1,0,2:T(8,128)S(1)} copy(f32[8,1024,130]{1,2,0:T(8,128)} %all-to-all-done) | data formatting | bytes 8519680 | tf_op jit(solution)/shard_map/all_to_all | solution.py:182
  159.0 0.3 pad.3
  159.3 3.9 %copy.114 = f32[17,8,8,1024]{3,1,2,0:T(8,128)S(1)} copy(f32[17,8,8,1024]{3,2,1,0:T(8,128)S(1)} %bitcast.177) | data formatting | bytes 8912896
  163.2 2.4 slice.20
  165.5 0.2 slice_reduce_fusion.1
  165.8 7.9 %copy.115 = f32[16,8,8,1024]{3,2,1,0:T(8,128)} copy(f32[16,8,8,1024]{3,1,2,0:T(8,128)} %bitcast.181) | data formatting | bytes 8388608
  173.7 3.7 %fusion.26 = f32[1024,128]{0,1:T(8,128)S(1)} fusion(f32[16,8,8,1024]{3,2,1,0:T(8,128)} %copy.115, f32[8,1024]{1,0:T(8,128)S(1)} %subtract_exponential_fusion.2), kind=kLoop, calls=%fused_computation.30 | loop fusion | flops 1966080 | bytes 4751360 | tf_op jit(solution)/shard_map/reduce_sum | solution.py:190
  177.5 0.2 copy.91
  177.7 3.9 %fusion.68 = bf16[1024,1,128]{2,0,1:T(8,128)(2,1)} fusion(bf16[1024,128]{1,0:T(8,128)(2,1)S(1)} %copy-done.8, f32[1024,1024]{0,1:T(8,128)} %copy-done.1, f32[1024]{0:T(1024)S(1)} %get-tuple-element.109, f32[1024,128]{1,0:T(8,128)S(1)} %copy.91, f32[1024]{0:T(1024)S(1)} %get-tuple-element.101, f32[1024]{0:T(1024)S(1)} %get-tuple-element.103, ...), kind=kOutput, calls=%fused_computation.57 | convolution fusion | flops 271187968 | bytes 5259264 | tf_op jit(solution)/shard_map/while/body/eval_jaxpr/hqk,khd->qhd/dot_general | solution.py:110
  181.7 7.1 %all-to-all-start.1 = ((bf16[16,64,128]{2,1,0:T(8,128)(2,1)}), bf16[16,64,128]{2,1,0:T(8,128)(2,1)S(1)}, u32[]{:S(2)}, u32[]{:S(2)}) async-start(bf16[16,64,128]{2,1,0:T(8,128)(2,1)} %bitcast.22), calls=%async_computation.1 | async-start | bytes 524288 | tf_op jit(solution)/shard_map/all_to_all | solution.py:201
  188.7 0.2 select_reduce_fusion
  188.9 8.3 %all-to-all-done.1 = bf16[16,64,128]{2,1,0:T(8,128)(2,1)S(1)} async-done(((bf16[16,64,128]{2,1,0:T(8,128)(2,1)}), bf16[16,64,128]{2,1,0:T(8,128)(2,1)S(1)}, u32[]{:S(2)}, u32[]{:S(2)}) %all-to-all-start.1) | async-done | bytes 262176 | tf_op jit(solution)/shard_map/all_to_all | solution.py:201
  197.2 5.1 %multiply_reduce_fusion = (f32[64]{0:T(128)S(1)}, f32[64,2048]{1,0:T(8,128)S(1)}) fusion(bf16[2048,2048]{1,0:T(8,128)(2,1)} %all-gather.5.cloned.1.call-done, bf16[64,2048]{1,0:T(8,128)(2,1)S(1)} %copy-done.2, bf16[16,64,128]{2,1,0:T(8,128)(2,1)S(1)} %all-to-all-done.1), kind=kOutput, calls=%fused_computation.61 | convolution fusion | flops 537395136 | bytes 9437440 | tf_op jit(solution)/shard_map/dot_general | solution.py:202
  202.3 0.8 convolution_convert_fusion
  203.1 30.3 %all_to_all.35 = bf16[32,16,2048]{2,1,0:T(8,128)(2,1)S(1)} all-to-all(bf16[32,16,2048]{2,1,0:T(8,128)(2,1)S(1)} %bitcast.183), channel_id=1, replica_groups=mesh['req'=8,'exp'=16] {'exp'}, dimensions={0} | all-to-all | bytes 4194304 | tf_op jit(solution)/shard_map/all_to_all | solution.py:222
  233.4 5.6 %fusion.24 = f32[2,16,16,704]{3,2,1,0:T(8,128)} fusion(bf16[2,2048,704]{1,2,0:T(8,128)(2,1)} %param.29, bf16[16,2,16,2048]{3,2,1,0:T(8,128)(2,1)S(1)} %bitcast.185), kind=kOutput, calls=%fused_computation.25 | convolution fusion | flops 1476395008 | bytes 9306112 | tf_op jit(solution)/shard_map/secd,edf->secf/dot_general | solution.py:225
  239.0 9.7 %fusion.32 = bf16[16,2,16,2048]{3,2,0,1:T(8,128)(2,1)} fusion(bf16[2,704,2048]{2,1,0:T(8,128)(2,1)} %param.31, f32[2,16,16,704]{3,2,1,0:T(8,128)} %fusion.24, bf16[2,2048,704]{1,2,0:T(8,128)(2,1)} %param.30, bf16[16,2,16,2048]{3,2,1,0:T(8,128)(2,1)S(1)} %bitcast.186), kind=kOutput, calls=%fused_computation.37 | convolution fusion | flops 2956001280 | bytes 17170432 | tf_op jit(solution)/shard_map/secf,efd->secd/dot_general | solution.py:228
  248.8 1.7 copy.99
  250.5 29.5 %all_to_all.36 = bf16[32,16,2048]{2,1,0:T(8,128)(2,1)S(1)} all-to-all(bf16[32,16,2048]{2,1,0:T(8,128)(2,1)S(1)} %bitcast.184), channel_id=1, replica_groups=mesh['req'=8,'exp'=16] {'exp'}, dimensions={0} | all-to-all | bytes 4194304 | tf_op jit(solution)/shard_map/all_to_all | solution.py:229
  280.0 1.2 fusion.35
  (80 shorter events, 0.8 us)
Async XLA Ops:
  6.5 96.9 %copy-start = (bf16[1024,128]{1,0:T(8,128)(2,1)S(1)}, bf16[1024,128]{1,0:T(8,128)(2,1)}, u32[]{:S(2)}) copy-start(bf16[1024,128]{1,0:T(8,128)(2,1)} %param.18) | copy-start | bytes 786436
  6.5 30.2 %all-gather.3.cloned.1.call-start = ((), (), s32[]{:S(2)}) async-start(), calls=%async_computation.4 | async-start | bytes 2359296 | tf_op jit(solution)/shard_map/all_gather | solution.py:176
  7.3 190.0 %all-gather.5.cloned.1.call-start = ((), (), s32[]{:S(2)}) async-start(), calls=%async_computation.5 | async-start | bytes 8912896 | tf_op jit(solution)/shard_map/all_gather | solution.py:200
  39.1 1.7 copy-start.7
  46.0 1.7 copy-start.7
  52.9 1.7 copy-start.7
  59.8 1.7 copy-start.7
  66.7 1.7 copy-start.7
  73.6 1.7 copy-start.7
  80.5 1.7 copy-start.7
  87.5 1.7 copy-start.7
  97.0 4.8 %copy-start.4 = (s32[64,4]{0,1:T(4,128)S(1)}, s32[64,4]{0,1:T(4,128)}, u32[]{:S(2)}) copy-start(s32[64,4]{0,1:T(4,128)} %param.27) | copy-start | bytes 3076
  97.0 6.4 %copy-start.6 = (bf16[64,4]{0,1:T(4,128)(2,1)S(1)}, bf16[64,4]{0,1:T(4,128)(2,1)}, u32[]{:S(2)}) copy-start(bf16[64,4]{0,1:T(4,128)(2,1)} %param.28) | copy-start | bytes 1540
  97.0 6.4 %copy-start.5 = (bf16[2048]{0:T(1024)(128)(2,1)S(1)}, bf16[2048]{0:T(1024)(128)(2,1)}, u32[]{:S(2)}) copy-start(bf16[2048]{0:T(1024)(128)(2,1)} %param.26) | copy-start | bytes 12292
  97.0 6.5 %copy-start.3 = (bf16[1024,128]{1,0:T(8,128)(2,1)S(1)}, bf16[1024,128]{1,0:T(8,128)(2,1)}, u32[]{:S(2)}) copy-start(bf16[1024,128]{1,0:T(8,128)(2,1)} %param.17) | copy-start | bytes 786436
  97.0 57.3 %all-to-all-start = ((f32[8,1024,130]{1,2,0:T(8,128)}), f32[8,1024,130]{1,2,0:T(8,128)}, u32[]{:S(2)}, u32[]{:S(2)}) async-start(f32[8,1024,130]{1,2,0:T(8,128)} %pad_maximum_fusion), calls=%async_computation | async-start | bytes 8912896 | tf_op jit(solution)/shard_map/all_to_all | solution.py:182
  104.5 2.0 copy-start.1
  173.7 4.0 %copy-start.8 = (bf16[1024,128]{1,0:T(8,128)(2,1)S(1)}, bf16[1024,128]{1,0:T(8,128)(2,1)}, u32[]{:S(2)}) copy-start(bf16[1024,128]{1,0:T(8,128)(2,1)} %param.19) | copy-start | bytes 786436
  177.4 19.8 %copy-start.2 = (bf16[64,2048]{1,0:T(8,128)(2,1)S(1)}, bf16[64,2048]{1,0:T(8,128)(2,1)}, u32[]{:S(2)}) copy-start(bf16[64,2048]{1,0:T(8,128)(2,1)} %param.24) | copy-start | bytes 786436
  181.7 15.6 %all-to-all-start.1 = ((bf16[16,64,128]{2,1,0:T(8,128)(2,1)}), bf16[16,64,128]{2,1,0:T(8,128)(2,1)S(1)}, u32[]{:S(2)}, u32[]{:S(2)}) async-start(bf16[16,64,128]{2,1,0:T(8,128)(2,1)} %bitcast.22), calls=%async_computation.1 | async-start | bytes 524288 | tf_op jit(solution)/shard_map/all_to_all | solution.py:201
Sparse Core Ops, SparseCore 0:
  9.1 27.5 all-gather.2
  38.8 71.1 all-gather.4
where the time goes:
time: 289 us; the launch traced here: 288 us
  blocking collectives  73 us (25%)
  waiting for transfers between devices  69.9 us (24%)
  matrix products  68.5 us (24%)
  other arithmetic  26.5 us (9%)
  local copies, waits for them, and re-layouts  24.2 us (8%)
  between operations  13.7 us (5%)
  starting transfers between devices  11.9 us (4%)
    all_to_all x1, waiting for transfers between devices, per_device(): lax.all_to_all(partial_value, 'req', split_axis=0, concat_axis=0, tiled=T...  47.1 us
    all_to_all x1, blocking collectives, per_device(): lax.all_to_all(buffer, 'exp', split_axis=0, concat_axis=0, tiled=True)  30.3 us
    all_to_all x1, blocking collectives, per_device(): lax.all_to_all(expert_out.astype(jnp.bfloat16).reshape(EXPERTS, slots, re...  29.5 us
    dot_general x8, matrix products, per_block(): jnp.einsum('hqgk,gkhd->qhd', exp_terms.astype(jnp.bfloat16), val_grid, pr...  22 us
    dot_general x8, matrix products, per_block(): jnp.einsum('qhd,gkhd->hqgk', query_grid, key_grid, preferred_element_type...  19.1 us
    unnamed x20, local copies, waits for them, and re-layouts  14.2 us
    reduce_sum x8, other arithmetic, per_block(): totals = jnp.sum(exp_terms, axis=(2, 3))  13.7 us
    all_gather x1, blocking collectives, per_device(): all_groups = lax.all_gather(tok_group, 'req', axis=0, tiled=True)  13.3 us
  transfers between devices with their start and end apart: 4, of which 3 were waited for; matrix products, arithmetic and copies ran while one was open for 32% of the time, Pallas kernels for 0%

commit v1 on v0

--- a/solution.py
+++ b/solution.py
@@ -170,7 +170,10 @@
     tok_dev = residual.shape[0]
     request, position, tok_group = token_layout(lengths, groups)
     request, position, tok_group = (request[0], position[0], tok_group[0])
-    all_groups = lax.all_gather(tok_group, "req", axis=0, tiled=True)
+    size = lax.axis_size("req")
+    shards = jnp.stack([tok_group for _ in range(size)])
+    shards = lax.all_to_all(shards, "req", split_axis=0, concat_axis=0)
+    all_groups = jnp.concatenate(shards, axis=0)
     partial_value = pack_parts(
         attend_prefix(
             lax.all_gather(queries, "req", axis=0, tiled=True),

time: 289 us -> 289 us (level)
  blocking collectives: 73 us -> 59.8 us
  waiting for transfers between devices: 69.9 us -> 78.2 us
  starting transfers between devices: 11.9 us -> 16.3 us
    all_gather x1 -> x0, blocking collectives: 13.3 us -> none  [per_device(): all_groups = lax.all_gather(tok_group, 'req', axis=0, tiled=True)]
    all_to_all x0 -> x1, waiting for transfers between devices: none -> 4.67 us  [per_device(): shards = lax.all_to_all(shards, 'req', split_axis=0, concat_axis=0)]
    all_to_all x0 -> x1, starting transfers between devices: none -> 4.38 us  [per_device(): shards = lax.all_to_all(shards, 'req', split_axis=0, concat_axis=0)]
    all_gather x1, waiting for transfers between devices: 13.1 us -> 16.6 us  [per_device(): lax.all_gather(queries, 'req', axis=0, tiled=True)]
    unnamed x20 -> x21, local copies, waits for them, and re-layouts: 14.2 us -> 14.2 us
  transfers between devices with their start and end apart: 4 -> 5, of which waited for: 3 -> 4; matrix products, arithmetic and copies ran while one was open for 32% -> 33% of each run, Pallas kernels for 0% -> 0%
where the time goes in v1:
time: 289 us; the launch traced here: 288 us
  waiting for transfers between devices  78.2 us (27%)
  matrix products  68.5 us (24%)
  blocking collectives  59.8 us (21%)
  other arithmetic  26.5 us (9%)
  local copies, waits for them, and re-layouts  24.9 us (9%)
  starting transfers between devices  16.3 us (6%)
  between operations  13.7 us (5%)
    all_to_all x1, waiting for transfers between devices, per_device(): lax.all_to_all(partial_value, 'req', split_axis=0, concat_axis=0, tiled=T...  47.1 us
    all_to_all x1, blocking collectives, per_device(): lax.all_to_all(buffer, 'exp', split_axis=0, concat_axis=0, tiled=True)  30.3 us
    all_to_all x1, blocking collectives, per_device(): lax.all_to_all(expert_out.astype(jnp.bfloat16).reshape(EXPERTS, slots, re...  29.5 us
    dot_general x8, matrix products, per_block(): jnp.einsum('hqgk,gkhd->qhd', exp_terms.astype(jnp.bfloat16), val_grid, pr...  22 us
    dot_general x8, matrix products, per_block(): jnp.einsum('qhd,gkhd->hqgk', query_grid, key_grid, preferred_element_type...  19.1 us
    all_gather x1, waiting for transfers between devices, per_device(): lax.all_gather(queries, 'req', axis=0, tiled=True)  16.6 us
    unnamed x21, local copies, waits for them, and re-layouts  14.2 us
    reduce_sum x8, other arithmetic, per_block(): totals = jnp.sum(exp_terms, axis=(2, 3))  13.7 us
  transfers between devices with their start and end apart: 5, of which 4 were waited for; matrix products, arithmetic and copies ran while one was open for 33% of the time, Pallas kernels for 0%

profile of v1, /device:TPU:0, one launch (start us, length us, event | category | flops | bytes accessed | tf_op | source)
XLA Modules:
  0.0 288.0 jit_solution(17721634932841118999)
XLA Ops:
  6.5 0.7 all-gather.3.cloned.1.call-update
  7.3 0.8 reduce_window_sum.24
  8.2 0.7 subtract_bitcast_fusion
  8.8 0.7 select_reduce_fusion.2
  9.6 0.6 stack.3
  10.2 4.4 %all-to-all-start = ((s32[8,1,1024]{2,1,0:T(1,128)}), s32[8,1,1024]{2,1,0:T(1,128)S(1)}, u32[]{:S(2)}, u32[]{:S(2)}) async-start(s32[8,1,1024]{2,1,0:T(1,128)} %stack.3), calls=%async_computation | async-start | bytes 65536 | tf_op jit(solution)/shard_map/all_to_all | solution.py:175
  14.6 0.7 all-gather.5.cloned.1.call-update
  15.4 4.7 %all-to-all-done = s32[8,1,1024]{2,1,0:T(1,128)S(1)} async-done(((s32[8,1,1024]{2,1,0:T(1,128)}), s32[8,1,1024]{2,1,0:T(1,128)S(1)}, u32[]{:S(2)}, u32[]{:S(2)}) %all-to-all-start) | async-done | bytes 32800 | tf_op jit(solution)/shard_map/all_to_all | solution.py:175
  20.1 16.6 %all-gather.3.cloned.1.call-done = bf16[8192,128]{1,0:T(8,128)(2,1)} async-done(((bf16[1024,128]{1,0:T(8,128)(2,1)}), bf16[8192,128]{1,0:T(8,128)(2,1)}) %all-gather.3.cloned.1.call-update) | async-done | bytes 2097168 | tf_op jit(solution)/shard_map/all_gather | solution.py:179
  36.7 55.3 %while.2 = (s32[]{:T(128)}, f32[8,1024,128]{1,2,0:T(8,128)}, f32[8,1024,1]{1,2,0:T(1,128)S(1)}, f32[8,1024,1]{1,2,0:T(1,128)S(1)}, s32[8,1024]{1,0:T(8,128)S(1)}...) while((s32[]{:T(128)}, f32[8,1024,128]{1,2,0:T(8,128)}, ...), condition=%wide.region_6.7_spmd, body=%wide.region_3.6_spmd.sunk | while | flops 1096812544 | bytes 29160576 | solution.py:76
  36.7 2.4 fusion.102
  39.1 1.7 fusion.104
  40.9 2.8 fusion.103
  43.6 2.4 fusion.102
  46.1 1.7 fusion.104
  47.8 2.7 fusion.103
  50.5 2.4 fusion.102
  53.0 1.7 fusion.104
  54.7 2.7 fusion.103
  57.5 2.4 fusion.102
  59.9 1.7 fusion.104
  61.6 2.7 fusion.103
  64.3 2.4 fusion.102
  66.8 1.7 fusion.104
  68.5 2.7 fusion.103
  71.2 2.4 fusion.102
  73.6 1.7 fusion.104
  75.4 2.8 fusion.103
  78.2 2.4 fusion.102
  80.6 1.7 fusion.104
  82.3 2.8 fusion.103
  85.1 2.4 fusion.102
  87.5 1.7 fusion.104
  89.2 2.8 fusion.103
  92.0 4.9 %pad_maximum_fusion = f32[8,1024,130]{1,2,0:T(8,128)} fusion(f32[8,1024,1]{1,2,0:T(1,128)S(1)} %get-tuple-element.78, f32[8,1024,1]{1,2,0:T(1,128)S(1)} %get-tuple-element.77, f32[8,1024,128]{1,2,0:T(8,128)} %get-tuple-element.76), kind=kLoop, calls=%fused_computation.27 | loop fusion | flops 2129920 | bytes 8519680 | tf_op jit(solution)/shard_map/concatenate | solution.py:34
  97.0 4.8 %all-to-all-start.1 = ((f32[8,1024,130]{1,2,0:T(8,128)}), f32[8,1024,130]{1,2,0:T(8,128)}, u32[]{:S(2)}, u32[]{:S(2)}) async-start(f32[8,1024,130]{1,2,0:T(8,128)} %pad_maximum_fusion), calls=%async_computation.1 | async-start | bytes 8912896 | tf_op jit(solution)/shard_map/all_to_all | solution.py:185
  102.0 0.1 eq.109
  102.1 0.8 reduce-window.6
  102.8 0.2 slice_reduce_fusion
  103.2 0.1 reduce_sum.112
  103.4 1.1 fusion.86
  104.5 2.0 copy-done.1
  106.5 0.6 fusion.27
  107.1 47.1 %all-to-all-done.1 = f32[8,1024,130]{1,2,0:T(8,128)} async-done(((f32[8,1024,130]{1,2,0:T(8,128)}), f32[8,1024,130]{1,2,0:T(8,128)}, u32[]{:S(2)}, u32[]{:S(2)}) %all-to-all-start.1) | async-done | bytes 4259872 | tf_op jit(solution)/shard_map/all_to_all | solution.py:185
  154.2 4.7 %copy.134 = f32[8,1024,130]{1,0,2:T(8,128)S(1)} copy(f32[8,1024,130]{1,2,0:T(8,128)} %all-to-all-done.1) | data formatting | bytes 8519680 | tf_op jit(solution)/shard_map/all_to_all | solution.py:185
  159.0 0.3 pad.3
  159.3 3.9 %copy.115 = f32[17,8,8,1024]{3,1,2,0:T(8,128)S(1)} copy(f32[17,8,8,1024]{3,2,1,0:T(8,128)S(1)} %bitcast.180) | data formatting | bytes 8912896
  163.2 2.4 slice.20
  165.5 0.2 slice_reduce_fusion.1
  165.8 7.9 %copy.116 = f32[16,8,8,1024]{3,2,1,0:T(8,128)} copy(f32[16,8,8,1024]{3,1,2,0:T(8,128)} %bitcast.184) | data formatting | bytes 8388608
  173.7 3.7 %fusion.26 = f32[1024,128]{0,1:T(8,128)S(1)} fusion(f32[16,8,8,1024]{3,2,1,0:T(8,128)} %copy.116, f32[8,1024]{1,0:T(8,128)S(1)} %subtract_exponential_fusion.2), kind=kLoop, calls=%fused_computation.30 | loop fusion | flops 1966080 | bytes 4751360 | tf_op jit(solution)/shard_map/reduce_sum | solution.py:193
  177.5 0.2 copy.91
  177.7 3.9 %fusion.68 = bf16[1024,1,128]{2,0,1:T(8,128)(2,1)} fusion(bf16[1024,128]{1,0:T(8,128)(2,1)S(1)} %copy-done.8, f32[1024,1024]{0,1:T(8,128)} %copy-done.1, f32[1024]{0:T(1024)S(1)} %get-tuple-element.109, f32[1024,128]{1,0:T(8,128)S(1)} %copy.91, f32[1024]{0:T(1024)S(1)} %get-tuple-element.101, f32[1024]{0:T(1024)S(1)} %get-tuple-element.103, ...), kind=kOutput, calls=%fused_computation.57 | convolution fusion | flops 271187968 | bytes 5259264 | tf_op jit(solution)/shard_map/while/body/eval_jaxpr/hqk,khd->qhd/dot_general | solution.py:110
  181.7 7.1 %all-to-all-start.2 = ((bf16[16,64,128]{2,1,0:T(8,128)(2,1)}), bf16[16,64,128]{2,1,0:T(8,128)(2,1)S(1)}, u32[]{:S(2)}, u32[]{:S(2)}) async-start(bf16[16,64,128]{2,1,0:T(8,128)(2,1)} %bitcast.22), calls=%async_computation.2 | async-start | bytes 524288 | tf_op jit(solution)/shard_map/all_to_all | solution.py:204
  188.7 0.2 select_reduce_fusion
  188.9 8.3 %all-to-all-done.2 = bf16[16,64,128]{2,1,0:T(8,128)(2,1)S(1)} async-done(((bf16[16,64,128]{2,1,0:T(8,128)(2,1)}), bf16[16,64,128]{2,1,0:T(8,128)(2,1)S(1)}, u32[]{:S(2)}, u32[]{:S(2)}) %all-to-all-start.2) | async-done | bytes 262176 | tf_op jit(solution)/shard_map/all_to_all | solution.py:204
  197.2 5.1 %multiply_reduce_fusion = (f32[64]{0:T(128)S(1)}, f32[64,2048]{1,0:T(8,128)S(1)}) fusion(bf16[2048,2048]{1,0:T(8,128)(2,1)} %all-gather.5.cloned.1.call-done, bf16[64,2048]{1,0:T(8,128)(2,1)S(1)} %copy-done.2, bf16[16,64,128]{2,1,0:T(8,128)(2,1)S(1)} %all-to-all-done.2), kind=kOutput, calls=%fused_computation.61 | convolution fusion | flops 537395136 | bytes 9437440 | tf_op jit(solution)/shard_map/dot_general | solution.py:205
  202.3 0.8 convolution_convert_fusion
  203.1 30.3 %all_to_all.44 = bf16[32,16,2048]{2,1,0:T(8,128)(2,1)S(1)} all-to-all(bf16[32,16,2048]{2,1,0:T(8,128)(2,1)S(1)} %bitcast.186), channel_id=1, replica_groups=mesh['req'=8,'exp'=16] {'exp'}, dimensions={0} | all-to-all | bytes 4194304 | tf_op jit(solution)/shard_map/all_to_all | solution.py:225
  233.4 5.6 %fusion.24 = f32[2,16,16,704]{3,2,1,0:T(8,128)} fusion(bf16[2,2048,704]{1,2,0:T(8,128)(2,1)} %param.29, bf16[16,2,16,2048]{3,2,1,0:T(8,128)(2,1)S(1)} %bitcast.188), kind=kOutput, calls=%fused_computation.25 | convolution fusion | flops 1476395008 | bytes 9306112 | tf_op jit(solution)/shard_map/secd,edf->secf/dot_general | solution.py:228
  239.0 9.7 %fusion.32 = bf16[16,2,16,2048]{3,2,0,1:T(8,128)(2,1)} fusion(bf16[2,704,2048]{2,1,0:T(8,128)(2,1)} %param.31, f32[2,16,16,704]{3,2,1,0:T(8,128)} %fusion.24, bf16[2,2048,704]{1,2,0:T(8,128)(2,1)} %param.30, bf16[16,2,16,2048]{3,2,1,0:T(8,128)(2,1)S(1)} %bitcast.189), kind=kOutput, calls=%fused_computation.37 | convolution fusion | flops 2956001280 | bytes 17170432 | tf_op jit(solution)/shard_map/secf,efd->secd/dot_general | solution.py:231
  248.8 1.7 copy.99
  250.5 29.5 %all_to_all.45 = bf16[32,16,2048]{2,1,0:T(8,128)(2,1)S(1)} all-to-all(bf16[32,16,2048]{2,1,0:T(8,128)(2,1)S(1)} %bitcast.187), channel_id=1, replica_groups=mesh['req'=8,'exp'=16] {'exp'}, dimensions={0} | all-to-all | bytes 4194304 | tf_op jit(solution)/shard_map/all_to_all | solution.py:232
  280.0 1.2 fusion.35
  (82 shorter events, 1.0 us)
Async XLA Ops:
  6.5 96.9 %copy-start = (bf16[1024,128]{1,0:T(8,128)(2,1)S(1)}, bf16[1024,128]{1,0:T(8,128)(2,1)}, u32[]{:S(2)}) copy-start(bf16[1024,128]{1,0:T(8,128)(2,1)} %param.18) | copy-start | bytes 786436
  6.5 30.2 %all-gather.3.cloned.1.call-start = ((), (), s32[]{:S(2)}) async-start(), calls=%async_computation.5 | async-start | bytes 2359296 | tf_op jit(solution)/shard_map/all_gather | solution.py:179
  10.2 9.8 %all-to-all-start = ((s32[8,1,1024]{2,1,0:T(1,128)}), s32[8,1,1024]{2,1,0:T(1,128)S(1)}, u32[]{:S(2)}, u32[]{:S(2)}) async-start(s32[8,1,1024]{2,1,0:T(1,128)} %stack.3), calls=%async_computation | async-start | bytes 65536 | tf_op jit(solution)/shard_map/all_to_all | solution.py:175
  14.6 182.6 %all-gather.5.cloned.1.call-start = ((), (), s32[]{:S(2)}) async-start(), calls=%async_computation.6 | async-start | bytes 8912896 | tf_op jit(solution)/shard_map/all_gather | solution.py:203
  39.1 1.7 copy-start.7
  46.0 1.7 copy-start.7
  52.9 1.7 copy-start.7
  59.8 1.7 copy-start.7
  66.7 1.7 copy-start.7
  73.6 1.7 copy-start.7
  80.5 1.7 copy-start.7
  87.5 1.7 copy-start.7
  97.0 4.8 %copy-start.4 = (s32[64,4]{0,1:T(4,128)S(1)}, s32[64,4]{0,1:T(4,128)}, u32[]{:S(2)}) copy-start(s32[64,4]{0,1:T(4,128)} %param.27) | copy-start | bytes 3076
  97.0 6.4 %copy-start.6 = (bf16[64,4]{0,1:T(4,128)(2,1)S(1)}, bf16[64,4]{0,1:T(4,128)(2,1)}, u32[]{:S(2)}) copy-start(bf16[64,4]{0,1:T(4,128)(2,1)} %param.28) | copy-start | bytes 1540
  97.0 6.4 %copy-start.5 = (bf16[2048]{0:T(1024)(128)(2,1)S(1)}, bf16[2048]{0:T(1024)(128)(2,1)}, u32[]{:S(2)}) copy-start(bf16[2048]{0:T(1024)(128)(2,1)} %param.26) | copy-start | bytes 12292
  97.0 6.5 %copy-start.3 = (bf16[1024,128]{1,0:T(8,128)(2,1)S(1)}, bf16[1024,128]{1,0:T(8,128)(2,1)}, u32[]{:S(2)}) copy-start(bf16[1024,128]{1,0:T(8,128)(2,1)} %param.17) | copy-start | bytes 786436
  97.0 57.3 %all-to-all-start.1 = ((f32[8,1024,130]{1,2,0:T(8,128)}), f32[8,1024,130]{1,2,0:T(8,128)}, u32[]{:S(2)}, u32[]{:S(2)}) async-start(f32[8,1024,130]{1,2,0:T(8,128)} %pad_maximum_fusion), calls=%async_computation.1 | async-start | bytes 8912896 | tf_op jit(solution)/shard_map/all_to_all | solution.py:185
  104.5 2.0 copy-start.1
  173.7 4.0 %copy-start.8 = (bf16[1024,128]{1,0:T(8,128)(2,1)S(1)}, bf16[1024,128]{1,0:T(8,128)(2,1)}, u32[]{:S(2)}) copy-start(bf16[1024,128]{1,0:T(8,128)(2,1)} %param.19) | copy-start | bytes 786436
  177.4 19.8 %copy-start.2 = (bf16[64,2048]{1,0:T(8,128)(2,1)S(1)}, bf16[64,2048]{1,0:T(8,128)(2,1)}, u32[]{:S(2)}) copy-start(bf16[64,2048]{1,0:T(8,128)(2,1)} %param.24) | copy-start | bytes 786436
  181.7 15.6 %all-to-all-start.2 = ((bf16[16,64,128]{2,1,0:T(8,128)(2,1)}), bf16[16,64,128]{2,1,0:T(8,128)(2,1)S(1)}, u32[]{:S(2)}, u32[]{:S(2)}) async-start(bf16[16,64,128]{2,1,0:T(8,128)(2,1)} %bitcast.22), calls=%async_computation.2 | async-start | bytes 524288 | tf_op jit(solution)/shard_map/all_to_all | solution.py:204
Sparse Core Ops, SparseCore 0:
  9.1 27.5 all-gather.2
  38.8 71.1 all-gather.4
